TPU v7x, 512 devices: a whole 4x4x16 slice. The times are simulated.
512 devices in a mesh: dp: 8 (over x, y_hi), mp: 64 (over z, y_lo, core).
Axes of the slice: x: 4, y: 4 (y_hi: 2, y_lo: 2; y = y_hi * 2 + y_lo), z: 16, core: 2. Of those that a mesh axis runs over, the one named last changes fastest.
Arguments:
- tokens: bfloat16 [4096, 16384], P('dp', 'mp'), may hold values from -6 to 6
- block_weight: bfloat16 [7, 256, 32768], P(None, None, 'mp'), may hold values from -0.125 to 0.125
- left_factor: bfloat16 [16384, 256], P('mp'), may hold values from -0.046875 to 0.046875
- right_factor: bfloat16 [256, 32768], P(None, 'mp'), may hold values from -0.375 to 0.375
- out_cotangent: bfloat16 [4096, 32768], P('dp', 'mp'), may hold values from -6 to 6
Outputs:
- activated: bfloat16 [4096, 32768], P('dp', 'mp')
- input_grad: bfloat16 [4096, 16384], P('dp', 'mp')
- weight_grad: bfloat16 [7, 256, 32768], P(None, 'dp', 'mp')
- left_grad: bfloat16 [16384, 256], P('mp')
- right_grad: bfloat16 [256, 32768], P(None, 'mp')
All inputs are finite; a program needn't handle non-finite values.
Results may differ from a plain program's by a relative error of at most 0.0062.
Values may be sent and summed in bfloat16 or wider, within the bound.
A program may use at most 64 MiB of HBM per device.

v0:
```python
import jax
import jax.numpy as jnp
from jax import lax
from jax.sharding import PartitionSpec as P

gelu_scale = 0.7978845608028654
gelu_cubic = 0.044715


def from_partner(shard, axis, distance):
    return lax.ppermute(shard, axis, [(i, i ^ 1 << distance) for i in range(lax.axis_size(axis))])


def gelu_parts(preact):
    inner = gelu_scale * (preact + gelu_cubic * preact * preact * preact)
    tangent = jnp.tanh(inner)
    value = 0.5 * preact * (1.0 + tangent)
    slope = 0.5 * (1.0 + tangent) + 0.5 * preact * (1.0 - tangent * tangent) * gelu_scale * (
        1.0 + 3.0 * gelu_cubic * preact * preact
    )
    return (value, slope)


def on_device(tokens, block_weight, left_factor, right_factor, out_cotangent):
    tok_rows = tokens.shape[0]
    local_width = tokens.shape[1]
    tap_count = block_weight.shape[0]
    block_size = block_weight.shape[1]
    hidden_local = block_weight.shape[2]
    group_count = local_width // block_size
    local_bits = group_count.bit_length() - 1
    tok_blocks = tokens.reshape(tok_rows, group_count, block_size)
    tap_inputs = [tok_blocks]
    for tap_index in range(1, tap_count):
        level_bit = tap_index - 1
        partner = from_partner(tokens, "mp", level_bit - local_bits)
        tap_inputs.append(partner.reshape(tok_rows, group_count, block_size))
    stacked = jnp.stack(tap_inputs, axis=2)
    weight_view = block_weight.reshape(tap_count, block_size, group_count, 2 * block_size)
    butterfly = jnp.einsum(
        "tgkc,kcgh->tgh", stacked, weight_view, preferred_element_type=jnp.float32
    )
    butterfly = butterfly.reshape(tok_rows, hidden_local)
    latent = lax.psum(jnp.dot(tokens, left_factor, preferred_element_type=jnp.float32), "mp")
    latent_bf = latent.astype(jnp.bfloat16)
    preact = butterfly + jnp.dot(latent_bf, right_factor, preferred_element_type=jnp.float32)
    value, slope = gelu_parts(preact)
    activated = value.astype(jnp.bfloat16)
    grad_pre = (out_cotangent.astype(jnp.float32) * slope).astype(jnp.bfloat16)
    latent_term = lax.dot_general(
        grad_pre, right_factor, (((1,), (1,)), ((), ())), preferred_element_type=jnp.float32
    )
    latent_grad = lax.psum(latent_term, "mp").astype(jnp.bfloat16)
    left_part = lax.dot_general(
        tokens, latent_grad, (((0,), (0,)), ((), ())), preferred_element_type=jnp.float32
    )
    right_part = lax.dot_general(
        latent_bf, grad_pre, (((0,), (0,)), ((), ())), preferred_element_type=jnp.float32
    )
    left_sum, right_sum = lax.psum((left_part, right_part), "dp")
    grad_view = grad_pre.reshape(tok_rows, group_count, 2 * block_size)
    spread = jnp.einsum(
        "tgh,kcgh->tgkc", grad_view, weight_view, preferred_element_type=jnp.float32
    )
    input_sum = spread[:, :, 0]
    for tap_index in range(1, tap_count):
        level_bit = tap_index - 1
        piece = spread[:, :, tap_index]
        returned = from_partner(piece.reshape(tok_rows, local_width), "mp", level_bit - local_bits)
        input_sum = input_sum + returned.reshape(tok_rows, group_count, block_size)
    low_rank = lax.dot_general(
        latent_grad, left_factor, (((1,), (1,)), ((), ())), preferred_element_type=jnp.float32
    )
    input_grad = (input_sum.reshape(tok_rows, local_width) + low_rank).astype(jnp.bfloat16)
    partial_value = jnp.einsum(
        "tgkc,tgh->kcgh", stacked, grad_view, preferred_element_type=jnp.float32
    )
    partial_value = partial_value.reshape(tap_count, block_size, hidden_local)
    weight_grad = lax.psum_scatter(partial_value, "dp", scatter_dimension=1, tiled=True).astype(
        jnp.bfloat16
    )
    return (
        activated,
        input_grad,
        weight_grad,
        left_sum.astype(jnp.bfloat16),
        right_sum.astype(jnp.bfloat16),
    )


def solution(mesh):
    return jax.shard_map(
        on_device,
        mesh=mesh,
        in_specs=(P("dp", "mp"), P(None, None, "mp"), P("mp", None), P(None, "mp"), P("dp", "mp")),
        out_specs=(P("dp", "mp"), P("dp", "mp"), P(None, "dp", "mp"), P("mp", None), P(None, "mp")),
        check_vma=False,
    )
```

profile of v0, /device:TPU:96, one launch (start us, length us, event | category | flops | bytes accessed | tf_op | source)
XLA Modules:
  0.0 672.3 jit_solution(16432143400853700451)
XLA Ops:
  7.2 0.0 copy-start
  7.2 0.0 reduce-scatter.2.cloned.1.call-start
  7.2 13.2 %collective-permute-start.5 = (bf16[512,256]{1,0:T(8,128)(2,1)}, bf16[512,256]{1,0:T(8,128)(2,1)S(1)}, u32[]{:S(2)}, u32[]{:S(2)}) collective-permute-start(bf16[512,256]{1,0:T(8,128)(2,1)} %param.5), channel_id=1, source_target_pairs={{0,32},{1,33},{2,34},{3,35},{4,36},{5,37},{6,38},{7,39},{8,40},{9,... | collective-permute-start | bytes 786440 | tf_op jit(solution)/shard_map/ppermute | solution.py:11
  20.4 4.3 collective-permute-start.4
  24.7 3.4 collective-permute-start.3
  28.1 3.5 collective-permute-start.1
  31.6 1.9 collective-permute-start
  33.5 1.2 fusion.35
  34.7 231.5 %all-reduce.4 = bf16[512,256]{1,0:T(8,128)(2,1)S(1)} all-reduce(f32[512,256]{1,0:T(8,128)S(1)} %fusion.35), channel_id=1, replica_groups=mesh['dp'=8,'mp'=64] {'mp'}, use_global_device_ids=true, to_apply=%region_0.0 | all-reduce | flops 131072 | bytes 786432 | tf_op jit(solution)/shard_map/psum | solution.py:44
  266.2 0.3 fusion.38
  266.5 0.0 copy-start.5
  266.6 0.0 collective-permute-done
  266.6 2.1 collective-permute-start.2
  268.7 1.0 bitcast_dynamic-update-slice_fusion.5
  269.6 0.0 collective-permute-done.1
  269.6 1.0 bitcast_dynamic-update-slice_fusion.4
  270.6 6.9 %collective-permute-done.2 = bf16[512,256]{1,0:T(8,128)(2,1)S(1)} collective-permute-done((bf16[512,256]{1,0:T(8,128)(2,1)S(1)}, bf16[512,256]{1,0:T(8,128)(2,1)S(1)}, u32[]{:S(2)}, u32[]{:S(2)}) %collective-permute-start.2) | collective-permute-done | bytes 262176 | tf_op jit(solution)/shard_map/ppermute | solution.py:11
  277.5 0.0 collective-permute-done.3
  277.5 1.0 bitcast_dynamic-update-slice_fusion.2
  278.5 0.0 collective-permute-done.4
  278.5 1.0 bitcast_dynamic-update-slice_fusion.1
  279.5 0.0 collective-permute-done.5
  279.5 2.6 fusion.15
  282.1 3.0 convolution_bitcast_fusion
  285.0 5.4 copy.14
  290.4 0.0 reduce-scatter.2.cloned.1.call-update
  290.5 1.1 fusion.36
  291.6 1.1 convolution_bitcast_fusion.1
  292.8 1.9 slice_bitcast_fusion.5
  294.6 0.9 copy-done.1
  295.5 1.9 collective-permute-start.6
  297.5 5.7 collective-permute-start.11
  303.1 1.9 collective-permute-start.10
  305.1 8.5 %collective-permute-start.9 = (f32[512,256]{1,0:T(8,128)}, f32[512,256]{1,0:T(8,128)}, u32[]{:S(2)}, u32[]{:S(2)}) collective-permute-start(f32[512,256]{1,0:T(8,128)} %get-tuple-element.20), channel_id=1, source_target_pairs={{0,8},{1,9},{2,10},{3,11},{4,12},{5,13},{6,14},{7,15},{8,0},{9,1},... | collective-permute-start | bytes 1572872 | tf_op jit(solution)/shard_map/ppermute | solution.py:11
  313.6 0.0 copy-start.4
  313.6 4.1 collective-permute-start.8
  317.7 275.6 %all-reduce.5 = bf16[512,256]{1,0:T(8,128)(2,1)S(1)} all-reduce(f32[512,256]{1,0:T(8,128)} %fusion.36), channel_id=1, replica_groups=mesh['dp'=8,'mp'=64] {'mp'}, use_global_device_ids=true, to_apply=%region_1.0 | all-reduce | flops 131072 | bytes 786432 | tf_op jit(solution)/shard_map/psum | solution.py:53
  593.2 0.0 collective-permute-done.6
  593.2 6.3 collective-permute-start.7
  599.6 1.1 fusion.37
  600.7 0.3 convolution_bitcast_fusion.2
  601.0 58.9 %all-reduce.6 = (bf16[256,256]{0,1:T(8,128)(2,1)S(1)}, bf16[256,512]{1,0:T(8,128)(2,1)}) all-reduce(f32[256,256]{0,1:T(8,128)S(1)} %convolution_bitcast_fusion.2, f32[256,512]{1,0:T(8,128)} %fusion.37), channel_id=1, replica_groups=mesh['dp'=8,'mp'=64] {'dp'}, use_global_device_ids=true, to_apply=%region_3.0 | all-reduce | flops 196608 | bytes 1179648 | tf_op jit(solution)/shard_map/psum | solution.py:60
  659.9 0.8 copy.16
  660.6 0.0 collective-permute-done.9
  660.6 0.0 collective-permute-done.7
  660.7 3.0 fusion.23
  663.7 1.1 convert_element_type.33
  664.7 0.8 copy.15
  (15 shorter events, 0.1 us)
Async XLA Ops:
  7.2 272.4 %copy-start = (bf16[7,256,512]{2,1,0:T(8,128)(2,1)S(1)}, bf16[7,256,512]{2,1,0:T(8,128)(2,1)}, u32[]{:S(2)}) copy-start(bf16[7,256,512]{2,1,0:T(8,128)(2,1)} %param.6) | copy-start | bytes 5505028
  7.2 259.4 %copy-start.2 = (bf16[512,256]{1,0:T(8,128)(2,1)S(1)}, bf16[512,256]{1,0:T(8,128)(2,1)}, u32[]{:S(2)}) copy-start(bf16[512,256]{1,0:T(8,128)(2,1)} %param.5) | copy-start | bytes 786436
  7.2 259.0 %copy-start.3 = (bf16[256,512]{1,0:T(8,128)(2,1)S(1)}, bf16[256,512]{1,0:T(8,128)(2,1)}, u32[]{:S(2)}) copy-start(bf16[256,512]{1,0:T(8,128)(2,1)} %param.8) | copy-start | bytes 786436
  7.2 656.5 %reduce-scatter.2.cloned.1.call-start = ((), (), s32[]{:S(2)}) async-start(), calls=%async_computation.1 | async-start | bytes 4718592 | tf_op jit(solution)/shard_map/reduce_scatter | solution.py:79
  7.2 272.2 %collective-permute-start.5 = (bf16[512,256]{1,0:T(8,128)(2,1)}, bf16[512,256]{1,0:T(8,128)(2,1)S(1)}, u32[]{:S(2)}, u32[]{:S(2)}) collective-permute-start(bf16[512,256]{1,0:T(8,128)(2,1)} %param.5), channel_id=1, source_target_pairs={{0,32},{1,33},{2,34},{3,35},{4,36},{5,37},{6,38},{7,39},{8,40},{9,... | collective-permute-start | bytes 786440 | tf_op jit(solution)/shard_map/ppermute | solution.py:11
  20.4 258.1 %collective-permute-start.4 = (bf16[512,256]{1,0:T(8,128)(2,1)}, bf16[512,256]{1,0:T(8,128)(2,1)}, u32[]{:S(2)}, u32[]{:S(2)}) collective-permute-start(bf16[512,256]{1,0:T(8,128)(2,1)} %param.5), channel_id=1, source_target_pairs={{0,16},{1,17},{2,18},{3,19},{4,20},{5,21},{6,22},{7,23},{8,24},{9,... | collective-permute-start | bytes 786440 | tf_op jit(solution)/shard_map/ppermute | solution.py:11
  24.7 252.8 %collective-permute-start.3 = (bf16[512,256]{1,0:T(8,128)(2,1)}, bf16[512,256]{1,0:T(8,128)(2,1)}, u32[]{:S(2)}, u32[]{:S(2)}) collective-permute-start(bf16[512,256]{1,0:T(8,128)(2,1)} %param.5), channel_id=1, source_target_pairs={{0,8},{1,9},{2,10},{3,11},{4,12},{5,13},{6,14},{7,15},{8,0},{9,1},... | collective-permute-start | bytes 786440 | tf_op jit(solution)/shard_map/ppermute | solution.py:11
  28.1 241.6 %collective-permute-start.1 = (bf16[512,256]{1,0:T(8,128)(2,1)}, bf16[512,256]{1,0:T(8,128)(2,1)}, u32[]{:S(2)}, u32[]{:S(2)}) collective-permute-start(bf16[512,256]{1,0:T(8,128)(2,1)} %param.5), channel_id=1, source_target_pairs={{0,2},{1,3},{2,0},{3,1},{4,6},{5,7},{6,4},{7,5},{8,10},{9,11},{10,... | collective-permute-start | bytes 786440 | tf_op jit(solution)/shard_map/ppermute | solution.py:11
  31.6 235.0 %collective-permute-start = (bf16[512,256]{1,0:T(8,128)(2,1)}, bf16[512,256]{1,0:T(8,128)(2,1)}, u32[]{:S(2)}, u32[]{:S(2)}) collective-permute-start(bf16[512,256]{1,0:T(8,128)(2,1)} %param.5), channel_id=1, source_target_pairs={{0,1},{1,0},{2,3},{3,2},{4,5},{5,4},{6,7},{7,6},{8,9},{9,8},{10,11... | collective-permute-start | bytes 786440 | tf_op jit(solution)/shard_map/ppermute | solution.py:11
  266.5 13.0 %copy-start.5 = (bf16[512,512]{1,0:T(8,128)(2,1)S(1)}, bf16[512,512]{1,0:T(8,128)(2,1)}, u32[]{:S(2)}) copy-start(bf16[512,512]{1,0:T(8,128)(2,1)} %param.9) | copy-start | bytes 1572868
  266.6 10.9 %collective-permute-start.2 = (bf16[512,256]{1,0:T(8,128)(2,1)S(1)}, bf16[512,256]{1,0:T(8,128)(2,1)S(1)}, u32[]{:S(2)}, u32[]{:S(2)}) collective-permute-start(bf16[512,256]{1,0:T(8,128)(2,1)S(1)} %copy-done.2), channel_id=1, source_target_pairs={{0,4},{1,5},{2,6},{3,7},{4,0},{5,1},{6,2},{7,3},{8,12},{9,13},{10,... | collective-permute-start | bytes 786440 | tf_op jit(solution)/shard_map/ppermute | solution.py:11
  292.7 2.8 copy-start.1
  295.5 297.7 %collective-permute-start.6 = (f32[512,256]{1,0:T(8,128)}, f32[512,256]{1,0:T(8,128)}, u32[]{:S(2)}, u32[]{:S(2)}) collective-permute-start(f32[512,256]{1,0:T(8,128)} %get-tuple-element.17), channel_id=1, source_target_pairs={{0,1},{1,0},{2,3},{3,2},{4,5},{5,4},{6,7},{7,6},{8,9},{9,8},{10,11... | collective-permute-start | bytes 1572872 | tf_op jit(solution)/shard_map/ppermute | solution.py:11
  297.5 363.2 %collective-permute-start.11 = (f32[512,256]{1,0:T(8,128)}, f32[512,256]{1,0:T(8,128)}, u32[]{:S(2)}, u32[]{:S(2)}) collective-permute-start(f32[512,256]{1,0:T(8,128)} %get-tuple-element.18), channel_id=1, source_target_pairs={{0,32},{1,33},{2,34},{3,35},{4,36},{5,37},{6,38},{7,39},{8,40},{9,... | collective-permute-start | bytes 1572872 | tf_op jit(solution)/shard_map/ppermute | solution.py:11
  303.1 357.5 %collective-permute-start.10 = (f32[512,256]{1,0:T(8,128)}, f32[512,256]{1,0:T(8,128)}, u32[]{:S(2)}, u32[]{:S(2)}) collective-permute-start(f32[512,256]{1,0:T(8,128)} %get-tuple-element.19), channel_id=1, source_target_pairs={{0,16},{1,17},{2,18},{3,19},{4,20},{5,21},{6,22},{7,23},{8,24},{9,... | collective-permute-start | bytes 1572872 | tf_op jit(solution)/shard_map/ppermute | solution.py:11
  305.1 355.6 %collective-permute-start.9 = (f32[512,256]{1,0:T(8,128)}, f32[512,256]{1,0:T(8,128)}, u32[]{:S(2)}, u32[]{:S(2)}) collective-permute-start(f32[512,256]{1,0:T(8,128)} %get-tuple-element.20), channel_id=1, source_target_pairs={{0,8},{1,9},{2,10},{3,11},{4,12},{5,13},{6,14},{7,15},{8,0},{9,1},... | collective-permute-start | bytes 1572872 | tf_op jit(solution)/shard_map/ppermute | solution.py:11
  313.6 347.1 %copy-start.4 = (bf16[256,256]{1,0:T(8,128)(2,1)S(1)}, bf16[256,256]{1,0:T(8,128)(2,1)}, u32[]{:S(2)}) copy-start(bf16[256,256]{1,0:T(8,128)(2,1)} %param.7) | copy-start | bytes 393220
  313.6 347.0 %collective-permute-start.8 = (f32[512,256]{1,0:T(8,128)}, f32[512,256]{1,0:T(8,128)}, u32[]{:S(2)}, u32[]{:S(2)}) collective-permute-start(f32[512,256]{1,0:T(8,128)} %get-tuple-element.21), channel_id=1, source_target_pairs={{0,4},{1,5},{2,6},{3,7},{4,0},{5,1},{6,2},{7,3},{8,12},{9,13},{10,... | collective-permute-start | bytes 1572872 | tf_op jit(solution)/shard_map/ppermute | solution.py:11
  593.2 67.4 %collective-permute-start.7 = (f32[512,256]{1,0:T(8,128)}, f32[512,256]{1,0:T(8,128)}, u32[]{:S(2)}, u32[]{:S(2)}) collective-permute-start(f32[512,256]{1,0:T(8,128)} %get-tuple-element.22), channel_id=1, source_target_pairs={{0,2},{1,3},{2,0},{3,1},{4,6},{5,7},{6,4},{7,5},{8,10},{9,11},{10,... | collective-permute-start | bytes 1572872 | tf_op jit(solution)/shard_map/ppermute | solution.py:11
Sparse Core Ops, SparseCore 0:
  290.6 98.8 reduce-scatter.1
where the time goes:
time: 673 us; the launch traced here: 672 us
  blocking collectives  566 us (84%)
  starting transfers between devices  56.7 us (8%)
  between operations  14.3 us (2%)
  local copies, waits for them, and re-layouts  13.7 us (2%)
  matrix products  13.7 us (2%)
  waiting for transfers between devices  6.93 us (1%)
    psum x1, blocking collectives, on_device(): latent_grad = lax.psum(latent_term, 'mp').astype(jnp.bfloat16)  276 us
    psum x1, blocking collectives, on_device(): lax.psum(jnp.dot(tokens, left_factor, preferred_element_type=jnp.float32)...  232 us
    psum x1, blocking collectives, on_device(): left_sum, right_sum = lax.psum((left_part, right_part), 'dp')  58.9 us
    ppermute x12, starting transfers between devices, from_partner(): lax.ppermute(shard, axis, [(i, i ^ 1 << distance) for i in range(lax.axis...  56.7 us
  transfers between devices with their start and end apart: 13, of which 1 were waited for; matrix products, arithmetic and copies ran while one was open for 2% of the time, Pallas kernels for 0%

commit v1 on v0

v1 whole, which is shorter than its diff:
```python
import functools

import jax
import jax.numpy as jnp
from jax import lax
from jax.experimental import pallas as pl
from jax.experimental.pallas import tpu as pltpu
from jax.sharding import PartitionSpec as P

gelu_scale = 0.7978845608028654
gelu_cubic = 0.044715
F32 = jnp.float32
BF16 = jnp.bfloat16

AR_CORE, AR_Y, AG_Y, AG_CORE, LEG_UP, LEG_DOWN, FAR_UP, FAR_DOWN, HALF_A, HALF_B, TAP = range(11)


def gelu_parts(preact):
    inner = gelu_scale * (preact + gelu_cubic * preact * preact * preact)
    tangent = jnp.tanh(inner)
    value = 0.5 * preact * (1.0 + tangent)
    slope = 0.5 * (1.0 + tangent) + 0.5 * preact * (1.0 - tangent * tangent) * gelu_scale * (
        1.0 + 3.0 * gelu_cubic * preact * preact
    )
    return value, slope


def mm(a, b):
    return lax.dot_general(a, b, (((1,), (0,)), ((), ())), preferred_element_type=F32)


def mm_nt(a, b):
    return lax.dot_general(a, b, (((1,), (1,)), ((), ())), preferred_element_type=F32)


def mm_tn(a, b):
    return lax.dot_general(a, b, (((0,), (0,)), ((), ())), preferred_element_type=F32)


def kernel(
    Z, ND,
    tok_h, w_h, left_h, right_h, cot_h,
    act_h, ig_h, wg_h, lg_h, rg_h,
    tok_v, w_v, left_v, right_v, cot_v,
    acc, act_v, gp_v,
    part, rx_core, half, rx_y, z_send, z_recv, gathered, lat,
    taps, spread, relay, iacc, ig_v,
    wg_send, wg_recv, wg_out, rg_all, left_send, left_recv, left_out, lg_all,
    one_send, one_recv, zs_send, zs_recv, d_send, d_recv, local,
):
    T, C = tok_v.shape
    R, H = right_v.shape
    K = w_v.shape[0]
    T2, T4 = T // 2, T // 4
    RB = C // ND
    NC = R // 128
    top, second = K - 1, K - 2

    d = lax.axis_index("dp")
    m = lax.axis_index("mp")
    c = lax.rem(m, 2)
    y = lax.rem(lax.div(m, 2), 2)
    z = lax.div(m, 4)
    base = m - z * 4

    def flip(stride):
        return m + stride - 2 * stride * lax.rem(lax.div(m, stride), 2)

    def z_at(k):
        return base + 4 * lax.rem(z + k, Z)

    core_peer, y_peer = flip(1), flip(2)

    def to(src, dst, send, recv, **where):
        return pltpu.make_async_remote_copy(
            src_ref=src, dst_ref=dst, send_sem=send, recv_sem=recv,
            device_id=where, device_id_type=pl.DeviceIdType.MESH,
        )

    def one(ph, k, src, dst, peer):
        return to(src, dst, one_send.at[ph, k], one_recv.at[ph, k], mp=peer)

    barrier = pltpu.get_barrier_semaphore()

    def greet(**where):
        pl.semaphore_signal(barrier, inc=1, device_id=where, device_id_type=pl.DeviceIdType.MESH)

    @pl.loop(1, Z)
    def _(k):
        greet(mp=z_at(k))

    @pl.loop(1, ND)
    def _(k):
        greet(dp=lax.rem(d + k, ND))

    greet(mp=core_peer)
    greet(mp=y_peer)

    loads = [
        pltpu.make_async_copy(src, dst, local.at[i])
        for i, (src, dst) in enumerate(
            [(tok_h, tok_v), (left_h, left_v), (w_h, w_v), (right_h, right_v), (cot_h, cot_v)]
        )
    ]
    for load in loads:
        load.start()

    def ar_core(ph):
        return one(ph, AR_CORE, part.at[ph, 1 - c], rx_core.at[ph], core_peer)

    def ar_y(ph):
        return one(ph, AR_Y, half.at[ph, 1 - y], rx_y.at[ph], y_peer)

    def ag_y(ph):
        return one(ph, AG_Y, gathered.at[ph, c, y], gathered.at[ph, c, y], y_peer)

    def ag_core(ph):
        return one(ph, AG_CORE, gathered.at[ph, c], gathered.at[ph, c], core_peer)

    def z_scatter(ph, k):
        there = lax.rem(z + k, Z)
        return to(
            z_send.at[ph, there], z_recv.at[ph, z], zs_send.at[ph, 0, there], zs_recv.at[ph, 0, z],
            mp=z_at(k),
        )

    def z_scatter_in(ph, k):
        there = lax.rem(z + k, Z)
        return to(
            z_send.at[ph, there], z_recv.at[ph, there], zs_send.at[ph, 0, there],
            zs_recv.at[ph, 0, there], mp=z_at(k),
        )

    def z_gather(ph, k):
        there = lax.rem(z + k, Z)
        return to(
            gathered.at[ph, c, y, z], gathered.at[ph, c, y, z], zs_send.at[ph, 1, there],
            zs_recv.at[ph, 1, z], mp=z_at(k),
        )

    def z_gather_in(ph, k):
        there = lax.rem(z + k, Z)
        return to(
            gathered.at[ph, c, y, there], gathered.at[ph, c, y, there], zs_send.at[ph, 1, there],
            zs_recv.at[ph, 1, there], mp=z_at(k),
        )

    def tap_src(ph, t):
        return tok_h if ph == 0 else spread.at[t - 1]

    def leg(ph, up):
        rows = pl.ds(0 if up else T2, T2)
        return one(
            ph, LEG_UP if up else LEG_DOWN, tap_src(ph, top).at[rows], relay.at[ph, 0 if up else 1],
            z_at(Z // 4 if up else Z - Z // 4),
        )

    def far(ph, up):
        rows = pl.ds(0 if up else T2, T2)
        return one(
            ph, FAR_UP if up else FAR_DOWN, relay.at[ph, 0 if up else 1],
            taps.at[ph, top - 1, rows], z_at(Z // 4 if up else Z - Z // 4),
        )

    def half_tap(ph, which):
        rows = pl.ds(which * T2, T2)
        return one(
            ph, HALF_A + which, tap_src(ph, second).at[rows], taps.at[ph, second - 1, rows],
            flip(1 << (second - 1)),
        )

    def tap(ph, t):
        return one(ph, TAP + t - 1, tap_src(ph, t), taps.at[ph, t - 1], flip(1 << (t - 1)))

    near = list(range(second - 1, 2, -1))

    def after_core(ph):
        ar_core(ph).wait_recv()
        for i in range(2):
            rows = pl.ds(i * T4, T4)
            half[ph, i] = part[ph, c, rows] + rx_core[ph, rows]
        ar_y(ph).start()

    def after_y(ph):
        ar_y(ph).wait_recv()
        for rb in range(T4 // 16):
            rows = pl.ds(rb * 16, 16)
            total = (half[ph, y, rows] + rx_y[ph, rows]).astype(BF16)
            for ch in range(NC):
                z_send[ph, rb * NC + ch] = total[:, ch * 128 : (ch + 1) * 128]
        z_recv[ph, z] = z_send[ph, z]

        @pl.loop(1, Z)
        def _(k):
            z_scatter(ph, k).start()

    def after_scatter(ph):
        @pl.loop(1, Z)
        def _(k):
            z_scatter_in(ph, k).wait_recv()

        total = z_recv[ph, 0].astype(F32)
        for i in range(1, Z):
            total = total + z_recv[ph, i].astype(F32)
        gathered[ph, c, y, z] = total.astype(BF16)

        @pl.loop(1, Z)
        def _(k):
            z_gather(ph, k).start()

    def after_gather(ph):
        @pl.loop(1, Z)
        def _(k):
            z_gather_in(ph, k).wait_recv()

        ag_y(ph).start()
        one(ph, AG_Y, gathered.at[ph, c, 1 - y], gathered.at[ph, c, 1 - y], y_peer).wait_recv()
        ag_core(ph).start()
        one(ph, AG_CORE, gathered.at[ph, 1 - c], gathered.at[ph, 1 - c], core_peer).wait_recv()
        for i in range(2):
            for j in range(2):
                for rb in range(T4 // 16):
                    for ch in range(NC):
                        lat[ph, pl.ds(i * T2 + j * T4 + rb * 16, 16), pl.ds(ch * 128, 128)] = (
                            gathered[ph, i, j, rb * NC + ch]
                        )

    def forward_far(ph):
        for up in (True, False):
            leg(ph, up).wait_recv()
            far(ph, up).start()

    def wait_tap(ph, t):
        if t == top:
            far(ph, True).wait_recv()
            far(ph, False).wait_recv()
        elif t == second:
            half_tap(ph, 0).wait_recv()
            half_tap(ph, 1).wait_recv()
        else:
            tap(ph, t).wait_recv()

    loads[0].wait()
    loads[1].wait()
    partial = mm(tok_v[...], left_v[...])
    part[0, 0] = partial[:T2]
    part[0, 1] = partial[T2:]
    pl.semaphore_wait(barrier, Z - 1 + ND - 1 + 2)
    ar_core(0).start()
    leg(0, True).start()
    leg(0, False).start()
    after_core(0)
    tap(0, 1).start()
    tap(0, 2).start()
    loads[2].wait()
    acc[...] = mm(tok_v[...], w_v[0])
    after_y(0)
    half_tap(0, 0).start()
    forward_far(0)
    for t in (1, 2):
        wait_tap(0, t)
        acc[...] += mm(taps[0, t - 1], w_v[t])
    after_scatter(0)
    half_tap(0, 1).start()
    for t in near:
        tap(0, t).start()
    after_gather(0)
    loads[3].wait()
    acc[...] += mm(lat[0], right_v[...])
    for t in near[::-1] + [second, top]:
        wait_tap(0, t)
        acc[...] += mm(taps[0, t - 1], w_v[t])
    loads[4].wait()

    @pl.loop(0, T // 32)
    def _(i):
        rows = pl.ds(pl.multiple_of(i * 32, 32), 32)
        value, slope = gelu_parts(acc[rows])
        act_v[rows] = value.astype(BF16)
        gp_v[rows] = (cot_v[rows].astype(F32) * slope).astype(BF16)

    stores = [pltpu.make_async_copy(act_v, act_h, local.at[5])]
    stores[0].start()

    def fill(t):
        spread[t - 1] = mm_nt(gp_v[...], w_v[t]).astype(BF16)

    fill(top)
    partial = mm_nt(gp_v[...], right_v[...])
    part[1, 0] = partial[:T2]
    part[1, 1] = partial[T2:]
    leg(1, True).start()
    leg(1, False).start()
    fill(second)
    ar_core(1).start()
    fill(1)
    after_core(1)
    fill(2)
    tap(1, 1).start()
    after_y(1)
    half_tap(1, 0).start()
    tap(1, 2).start()

    for t in range(K):
        source = tok_v[...] if t == 0 else taps[0, t - 1]
        wg_send[:, t] = mm_tn(source, gp_v[...]).astype(BF16).reshape(ND, RB, H)
    wg_send[:, K] = mm_tn(lat[0], gp_v[...]).astype(BF16).reshape(ND, RB, H)

    def dp_copy(row, k, src, dst, incoming):
        there = lax.rem(d + k, ND)
        return to(
            src(there), dst(there if incoming else d), d_send.at[row, there],
            d_recv.at[row, there if incoming else d], dp=there,
        )

    def wg_copy(k, incoming=False):
        return dp_copy(0, k, lambda p: wg_send.at[p], lambda p: wg_recv.at[p], incoming)

    def rg_copy(k, incoming=False):
        return dp_copy(1, k, lambda p: wg_out.at[K], lambda p: rg_all.at[p], incoming)

    def ls_copy(k, incoming=False):
        return dp_copy(2, k, lambda p: left_send.at[p], lambda p: left_recv.at[p], incoming)

    def lg_copy(k, incoming=False):
        return dp_copy(3, k, lambda p: left_out, lambda p: lg_all.at[p], incoming)

    def start_all(make):
        @pl.loop(1, ND)
        def _(k):
            make(k).start()

    def receive_all(make):
        @pl.loop(1, ND)
        def _(k):
            make(k, True).wait_recv()

    wg_recv[d] = wg_send[d]
    start_all(wg_copy)
    for t in near:
        fill(t)
    forward_far(1)
    after_scatter(1)
    half_tap(1, 1).start()
    for t in near:
        tap(1, t).start()
    iacc[...] = mm_nt(gp_v[...], w_v[0])
    for t in (1, 2):
        wait_tap(1, t)
        iacc[...] += taps[1, t - 1].astype(F32)
    after_gather(1)
    left_send[...] = mm_tn(tok_v[...], lat[1]).astype(BF16).reshape(ND, RB, R)
    left_recv[d] = left_send[d]
    start_all(ls_copy)
    iacc[...] += mm_nt(lat[1], left_v[...])
    receive_all(wg_copy)

    @pl.loop(0, K + 1)
    def _(t):
        total = wg_recv[0, t].astype(F32)
        for i in range(1, ND):
            total = total + wg_recv[i, t].astype(F32)
        wg_out[t] = total.astype(BF16)

    rg_all[d] = wg_out[K]
    start_all(rg_copy)
    stores.append(pltpu.make_async_copy(wg_out.at[pl.ds(0, K)], wg_h, local.at[6]))
    stores[-1].start()
    receive_all(ls_copy)
    total = left_recv[0].astype(F32)
    for i in range(1, ND):
        total = total + left_recv[i].astype(F32)
    left_out[...] = total.astype(BF16)
    lg_all[d] = left_out[...]
    start_all(lg_copy)
    for t in near[::-1] + [second]:
        wait_tap(1, t)
        iacc[...] += taps[1, t - 1].astype(F32)
    receive_all(rg_copy)
    stores.append(pltpu.make_async_copy(rg_all, rg_h, local.at[7]))
    stores[-1].start()
    receive_all(lg_copy)
    stores.append(pltpu.make_async_copy(lg_all, lg_h, local.at[8]))
    stores[-1].start()
    wait_tap(1, top)
    ig_v[...] = (iacc[...] + taps[1, top - 1].astype(F32)).astype(BF16)
    stores.append(pltpu.make_async_copy(ig_v, ig_h, local.at[9]))
    stores[-1].start()

    for ph in range(2):
        for copy in (ar_core, ar_y, ag_y, ag_core):
            copy(ph).wait_send()
        for up in (True, False):
            leg(ph, up).wait_send()
            far(ph, up).wait_send()
        for which in range(2):
            half_tap(ph, which).wait_send()
        for t in [1, 2] + near:
            tap(ph, t).wait_send()

        @pl.loop(1, Z)
        def _(k):
            z_scatter(ph, k).wait_send()
            z_gather(ph, k).wait_send()

    @pl.loop(1, ND)
    def _(k):
        for copy in (wg_copy, rg_copy, ls_copy, lg_copy):
            copy(k).wait_send()

    for store in stores:
        store.wait()


def on_device(tokens, block_weight, left_factor, right_factor, out_cotangent):
    ND = lax.axis_size("dp")
    Z = lax.axis_size("mp") // 4
    T, C = tokens.shape
    K, _, H = block_weight.shape
    R = right_factor.shape[0]
    RB = C // ND
    any_spec = pl.BlockSpec(memory_space=pl.ANY)
    bf = lambda *shape: pltpu.VMEM(shape, BF16)
    fl = lambda *shape: pltpu.VMEM(shape, F32)
    dma = lambda *shape: pltpu.SemaphoreType.DMA(shape)
    out = lambda *shape: jax.ShapeDtypeStruct(shape, BF16)
    act, ig, wg, lg, rg = pl.pallas_call(
        functools.partial(kernel, Z, ND),
        out_shape=(out(T, H), out(T, C), out(K, RB, H), out(ND, RB, R), out(ND, RB, H)),
        in_specs=[any_spec] * 5,
        out_specs=[any_spec] * 5,
        scratch_shapes=[
            bf(T, C), bf(K, C, H), bf(C, R), bf(R, H), bf(T, H),
            fl(T, H), bf(T, H), bf(T, H),
            fl(2, 2, T // 2, R), fl(2, T // 2, R), fl(2, 2, T // 4, R), fl(2, T // 4, R),
            bf(2, Z, 16, 128), bf(2, Z, 16, 128), bf(2, 2, 2, Z, 16, 128), bf(2, T, R),
            bf(2, K - 1, T, C), bf(K - 1, T, C), bf(2, 2, T // 2, C), fl(T, C), bf(T, C),
            bf(ND, K + 1, RB, H), bf(ND, K + 1, RB, H), bf(K + 1, RB, H), bf(ND, RB, H),
            bf(ND, RB, R), bf(ND, RB, R), bf(RB, R), bf(ND, RB, R),
            dma(2, TAP + K - 1), dma(2, TAP + K - 1), dma(2, 2, Z), dma(2, 2, Z),
            dma(4, ND), dma(4, ND), dma(10),
        ],
        compiler_params=pltpu.CompilerParams(
            collective_id=0, has_side_effects=True, vmem_limit_bytes=56 * 1024 * 1024
        ),
    )(tokens, block_weight, left_factor, right_factor, out_cotangent)
    return act, ig, wg, lg.reshape(C, R), rg.reshape(R, H)


def solution(mesh):
    return jax.shard_map(
        on_device,
        mesh=mesh,
        in_specs=(P("dp", "mp"), P(None, None, "mp"), P("mp", None), P(None, "mp"), P("dp", "mp")),
        out_specs=(P("dp", "mp"), P("dp", "mp"), P(None, "dp", "mp"), P("mp", None), P(None, "mp")),
        check_vma=False,
    )
```

time: 673 us -> 154 us (0.23)
  the two profiles are of different devices: /device:TPU:96 before, /device:TPU:1 now
where the time goes in v1:
time: 154 us
  Pallas kernels  146 us (95%)
  local copies, waits for them, and re-layouts  6.59 us (4%)
    pallas_call x1, Pallas kernels, on_device(): pl.pallas_call(functools.partial(kernel, Z, ND), out_shape=(out(T, H), ou...  146 us
    unnamed x9, local copies, waits for them, and re-layouts  6.59 us

profile of v1, /device:TPU:1, one launch (start us, length us, event | category | flops | bytes accessed | tf_op | source)
XLA Modules:
  0.0 153.6 jit_solution(7862913245125452690)
XLA Ops:
  0.6 146.4 %shard_map.92 = (bf16[512,512]{1,0:T(8,128)(2,1)}, bf16[512,256]{1,0:T(8,128)(2,1)}, bf16[7,32,512]{2,1,0:T(8,128)(2,1)}, bf16[8,32,256]{2,1,0:T(8,128)(2,1)}, bf16[8,32,512]{2,1,0:T(8,128)(2,1)}) custom-call(bf16[512,256]{1,0:T(8,128)(2,1)} %tok_h.1, bf16[7,256,512]{2,1,0:T(8,128)(2,1)} %w_h.1, bf16[256,256]{1,0:T(8,128)(2,1)} %left_h.1, ...), custom_call_target="tpu_custom_call" | custom-call | tf_op jit(solution)/shard_map/pallas_call | solution.py:427
  147.0 0.0 copy-start.1
  147.0 0.0 copy-start
  147.0 1.9 %copy.15 = bf16[512,512]{1,0:T(8,128)(2,1)} copy(bf16[512,512]{1,0:T(8,128)(2,1)} %get-tuple-element.20) | data formatting | bytes 1048576
  148.9 1.7 %copy.16 = bf16[512,256]{1,0:T(8,128)(2,1)} copy(bf16[512,256]{1,0:T(8,128)(2,1)} %get-tuple-element.21) | data formatting | bytes 524288
  150.6 1.6 %copy.17 = bf16[7,32,512]{2,1,0:T(8,128)(2,1)} copy(bf16[7,32,512]{2,1,0:T(8,128)(2,1)} %get-tuple-element.22) | data formatting | bytes 458752
  152.2 0.0 copy-done.1
  152.2 0.7 copy.18
  152.9 0.0 copy-done
  152.9 0.7 copy.19
Async XLA Ops:
  147.0 5.2 %copy-start.1 = (bf16[8,32,256]{2,1,0:T(8,128)(2,1)S(1)}, bf16[8,32,256]{2,1,0:T(8,128)(2,1)}, u32[]{:S(2)}) copy-start(bf16[8,32,256]{2,1,0:T(8,128)(2,1)} %get-tuple-element.13) | copy-start | bytes 393220
  147.0 5.9 %copy-start = (bf16[8,32,512]{2,1,0:T(8,128)(2,1)S(1)}, bf16[8,32,512]{2,1,0:T(8,128)(2,1)}, u32[]{:S(2)}) copy-start(bf16[8,32,512]{2,1,0:T(8,128)(2,1)} %get-tuple-element.14) | copy-start | bytes 786436

commit v2 on v1

--- a/solution.py
+++ b/solution.py
@@ -12,7 +12,8 @@
 F32 = jnp.float32
 BF16 = jnp.bfloat16
 
-AR_CORE, AR_Y, AG_Y, AG_CORE, LEG_UP, LEG_DOWN, FAR_UP, FAR_DOWN, HALF_A, HALF_B, TAP = range(11)
+AR_CORE, AR_Y, AG_Y, AG_CORE, TAP_CORE, TAP_Y = range(6)
+NQ = 4
 
 
 def gelu_parts(preact):
@@ -43,18 +44,19 @@
     act_h, ig_h, wg_h, lg_h, rg_h,
     tok_v, w_v, left_v, right_v, cot_v,
     acc, act_v, gp_v,
-    part, rx_core, half, rx_y, z_send, z_recv, gathered, lat,
-    taps, spread, relay, iacc, ig_v,
+    part, rx_core, half, half_send, rx_y, z_send, z_recv, gathered, lat,
+    taps, near_out, near_in, own, chain_out, chain_in, iacc, ig_v,
     wg_send, wg_recv, wg_out, rg_all, left_send, left_recv, left_out, lg_all,
-    one_send, one_recv, zs_send, zs_recv, d_send, d_recv, local,
+    one_send, one_recv, zs_send, zs_recv, f_send, f_recv, b_send, b_recv, d_send, d_recv, local,
 ):
     T, C = tok_v.shape
     R, H = right_v.shape
     K = w_v.shape[0]
-    T2, T4 = T // 2, T // 4
+    T2, T4, TQ = T // 2, T // 4, T // NQ
     RB = C // ND
     NC = R // 128
-    top, second = K - 1, K - 2
+    nz = K - 3
+    top = nz - 1
 
     d = lax.axis_index("dp")
     m = lax.axis_index("mp")
@@ -109,7 +111,7 @@
         return one(ph, AR_CORE, part.at[ph, 1 - c], rx_core.at[ph], core_peer)
 
     def ar_y(ph):
-        return one(ph, AR_Y, half.at[ph, 1 - y], rx_y.at[ph], y_peer)
+        return one(ph, AR_Y, half_send.at[ph, 1 - y], rx_y.at[ph], y_peer)
 
     def ag_y(ph):
         return one(ph, AG_Y, gathered.at[ph, c, y], gathered.at[ph, c, y], y_peer)
@@ -145,47 +147,68 @@
             zs_recv.at[ph, 1, there], mp=z_at(k),
         )
 
-    def tap_src(ph, t):
-        return tok_h if ph == 0 else spread.at[t - 1]
-
-    def leg(ph, up):
-        rows = pl.ds(0 if up else T2, T2)
-        return one(
-            ph, LEG_UP if up else LEG_DOWN, tap_src(ph, top).at[rows], relay.at[ph, 0 if up else 1],
-            z_at(Z // 4 if up else Z - Z // 4),
-        )
-
-    def far(ph, up):
-        rows = pl.ds(0 if up else T2, T2)
-        return one(
-            ph, FAR_UP if up else FAR_DOWN, relay.at[ph, 0 if up else 1],
-            taps.at[ph, top - 1, rows], z_at(Z // 4 if up else Z - Z // 4),
-        )
-
-    def half_tap(ph, which):
-        rows = pl.ds(which * T2, T2)
-        return one(
-            ph, HALF_A + which, tap_src(ph, second).at[rows], taps.at[ph, second - 1, rows],
-            flip(1 << (second - 1)),
-        )
-
-    def tap(ph, t):
-        return one(ph, TAP + t - 1, tap_src(ph, t), taps.at[ph, t - 1], flip(1 << (t - 1)))
-
-    near = list(range(second - 1, 2, -1))
+    def near_tap(ph, k):
+        src = tok_h if ph == 0 else near_out.at[k]
+        dst = taps.at[k] if ph == 0 else near_in.at[k]
+        return one(ph, TAP_CORE + k, src, dst, flip(1 << k))
+
+    def rows_of(q):
+        return pl.ds(q * TQ, TQ)
+
+    def z_flip(at, k):
+        return at + (1 << k) - (2 << k) * lax.rem(lax.div(at, 1 << k), 2)
+
+    def way(at, k):
+        return lax.rem(lax.div(at, 1 << k), 2)
+
+    onward = z_flip(z_flip(z, top - 1), top)
+
+    def z_tap(s, q):
+        return to(
+            tok_h.at[rows_of(q)], taps.at[2 + s, rows_of(q)], f_send.at[s, q], f_recv.at[s, q],
+            mp=base + 4 * z_flip(z, s),
+        )
+
+    def z_pass(q):
+        return to(
+            taps.at[1 + top, rows_of(q)], taps.at[2 + top, rows_of(q)], f_send.at[top, q],
+            f_recv.at[top, q], mp=base + 4 * onward,
+        )
+
+    def pass_on(q):
+        z_tap(top - 1, q).wait_recv()
+        z_pass(q).start()
+
+    def arrived(s, q):
+        (z_pass(q) if s == top else z_tap(s, q)).wait_recv()
+
+    def term(s, q):
+        peer = onward if s == top else z_flip(z, s)
+        return to(
+            chain_out.at[s, rows_of(q)], chain_in.at[s, rows_of(q)], b_send.at[s, q],
+            b_recv.at[s, q], mp=base + 4 * peer,
+        )
+
+    def add_on(q):
+        term(top, q).wait_recv()
+        rows = rows_of(q)
+        chain_out[top - 1, rows] = (own[rows] + chain_in[top, rows].astype(F32)).astype(BF16)
+        term(top - 1, q).start()
 
     def after_core(ph):
         ar_core(ph).wait_recv()
         for i in range(2):
             rows = pl.ds(i * T4, T4)
-            half[ph, i] = part[ph, c, rows] + rx_core[ph, rows]
+            both = part[ph, c, rows] + rx_core[ph, rows]
+            half[ph, i] = both
+            half_send[ph, i] = both.astype(BF16)
         ar_y(ph).start()
 
     def after_y(ph):
         ar_y(ph).wait_recv()
         for rb in range(T4 // 16):
             rows = pl.ds(rb * 16, 16)
-            total = (half[ph, y, rows] + rx_y[ph, rows]).astype(BF16)
+            total = (half[ph, y, rows] + rx_y[ph, rows].astype(F32)).astype(BF16)
             for ch in range(NC):
                 z_send[ph, rb * NC + ch] = total[:, ch * 128 : (ch + 1) * 128]
         z_recv[ph, z] = z_send[ph, z]
@@ -214,8 +237,12 @@
             z_gather_in(ph, k).wait_recv()
 
         ag_y(ph).start()
+
+    def after_gather_y(ph):
         one(ph, AG_Y, gathered.at[ph, c, 1 - y], gathered.at[ph, c, 1 - y], y_peer).wait_recv()
         ag_core(ph).start()
+
+    def after_gather_core(ph):
         one(ph, AG_CORE, gathered.at[ph, 1 - c], gathered.at[ph, 1 - c], core_peer).wait_recv()
         for i in range(2):
             for j in range(2):
@@ -225,86 +252,96 @@
                             gathered[ph, i, j, rb * NC + ch]
                         )
 
-    def forward_far(ph):
-        for up in (True, False):
-            leg(ph, up).wait_recv()
-            far(ph, up).start()
-
-    def wait_tap(ph, t):
-        if t == top:
-            far(ph, True).wait_recv()
-            far(ph, False).wait_recv()
-        elif t == second:
-            half_tap(ph, 0).wait_recv()
-            half_tap(ph, 1).wait_recv()
-        else:
-            tap(ph, t).wait_recv()
-
     loads[0].wait()
     loads[1].wait()
     partial = mm(tok_v[...], left_v[...])
     part[0, 0] = partial[:T2]
     part[0, 1] = partial[T2:]
     pl.semaphore_wait(barrier, Z - 1 + ND - 1 + 2)
+    inner = way(z, top - 2) + way(z, top - 1) - 2 * way(z, top - 2) * way(z, top - 1)
+
+    def when_early(ph, queue, quarters):
+        @pl.when(inner == 1 - ph)
+        def _():
+            for q in quarters:
+                queue(q)
+
+    def when_late(ph, queue, quarters):
+        when_early(1 - ph, queue, quarters)
+
     ar_core(0).start()
-    leg(0, True).start()
-    leg(0, False).start()
+    z_tap(top - 1, 0).start()
     after_core(0)
-    tap(0, 1).start()
-    tap(0, 2).start()
+    near_tap(0, 0).start()
     loads[2].wait()
     acc[...] = mm(tok_v[...], w_v[0])
     after_y(0)
-    half_tap(0, 0).start()
-    forward_far(0)
-    for t in (1, 2):
-        wait_tap(0, t)
-        acc[...] += mm(taps[0, t - 1], w_v[t])
+    z_tap(top - 1, 1).start()
+    near_tap(0, 1).start()
+    pass_on(0)
     after_scatter(0)
-    half_tap(0, 1).start()
-    for t in near:
-        tap(0, t).start()
+    for q in range(2, NQ):
+        z_tap(top - 1, q).start()
+    for s in range(top - 1):
+        for q in range(NQ):
+            z_tap(s, q).start()
+    pass_on(1)
+    for k in range(2):
+        near_tap(0, k).wait_recv()
+        acc[...] += mm(taps[k], w_v[1 + k])
+    when_early(0, pass_on, (2, 3))
     after_gather(0)
+    when_late(0, pass_on, (2,))
     loads[3].wait()
+    loads[4].wait()
+    after_gather_y(0)
+    when_late(0, pass_on, (3,))
+    acc[...] += mm(taps[1 + top], w_v[2 + top])
+    after_gather_core(0)
     acc[...] += mm(lat[0], right_v[...])
-    for t in near[::-1] + [second, top]:
-        wait_tap(0, t)
-        acc[...] += mm(taps[0, t - 1], w_v[t])
-    loads[4].wait()
-
-    @pl.loop(0, T // 32)
-    def _(i):
-        rows = pl.ds(pl.multiple_of(i * 32, 32), 32)
-        value, slope = gelu_parts(acc[rows])
-        act_v[rows] = value.astype(BF16)
-        gp_v[rows] = (cot_v[rows].astype(F32) * slope).astype(BF16)
+    for s in range(top - 1):
+        for q in range(NQ):
+            arrived(s, q)
+        acc[...] += mm(taps[2 + s], w_v[3 + s])
+
+    stores = []
+    for q in range(NQ):
+        rows = rows_of(q)
+        arrived(top, q)
+        acc[rows] += mm(taps[2 + top, rows], w_v[3 + top])
+
+        @pl.loop(0, TQ // 32)
+        def _(i):
+            here = pl.ds(pl.multiple_of(q * TQ + i * 32, 32), 32)
+            value, slope = gelu_parts(acc[here])
+            act_v[here] = value.astype(BF16)
+            gp_v[here] = (cot_v[here].astype(F32) * slope).astype(BF16)
+
+        chain_out[top, rows] = mm_nt(gp_v[rows], w_v[3 + top]).astype(BF16)
+        if q == 0:
+            term(top, q).start()
 
     stores = [pltpu.make_async_copy(act_v, act_h, local.at[5])]
     stores[0].start()
-
-    def fill(t):
-        spread[t - 1] = mm_nt(gp_v[...], w_v[t]).astype(BF16)
-
-    fill(top)
     partial = mm_nt(gp_v[...], right_v[...])
     part[1, 0] = partial[:T2]
     part[1, 1] = partial[T2:]
-    leg(1, True).start()
-    leg(1, False).start()
-    fill(second)
     ar_core(1).start()
-    fill(1)
-    after_core(1)
-    fill(2)
-    tap(1, 1).start()
-    after_y(1)
-    half_tap(1, 0).start()
-    tap(1, 2).start()
-
-    for t in range(K):
-        source = tok_v[...] if t == 0 else taps[0, t - 1]
+
+    def fill(s):
+        chain_out[s] = mm_nt(gp_v[...], w_v[3 + s]).astype(BF16)
+
+    def fill_near(k):
+        near_out[k] = mm_nt(gp_v[...], w_v[1 + k]).astype(BF16)
+
+    def fill_weight(t):
+        if t == K:
+            source = lat[0]
+        elif t == 0:
+            source = tok_v[...]
+        else:
+            source = taps[t - 1]
         wg_send[:, t] = mm_tn(source, gp_v[...]).astype(BF16).reshape(ND, RB, H)
-    wg_send[:, K] = mm_tn(lat[0], gp_v[...]).astype(BF16).reshape(ND, RB, H)
 
     def dp_copy(row, k, src, dst, incoming):
         there = lax.rem(d + k, ND)
@@ -313,8 +350,16 @@
             d_recv.at[row, there if incoming else d], dp=there,
         )
 
-    def wg_copy(k, incoming=False):
-        return dp_copy(0, k, lambda p: wg_send.at[p], lambda p: wg_recv.at[p], incoming)
+    KH = (K + 1) // 2
+
+    def wg_copy(part_no, k, incoming=False):
+        planes = pl.ds(0, KH) if part_no == 0 else pl.ds(KH, K + 1 - KH)
+        return dp_copy(
+            4 * part_no, k, lambda p: wg_send.at[p, planes], lambda p: wg_recv.at[p, planes], incoming
+        )
+
+    wg_first = functools.partial(wg_copy, 0)
+    wg_second = functools.partial(wg_copy, 1)
 
     def rg_copy(k, incoming=False):
         return dp_copy(1, k, lambda p: wg_out.at[K], lambda p: rg_all.at[p], incoming)
@@ -335,25 +380,49 @@
         def _(k):
             make(k, True).wait_recv()
 
+    own[...] = mm_nt(gp_v[...], w_v[2 + top])
+    after_core(1)
+    fill_near(0)
+    near_tap(1, 0).start()
+    fill_near(1)
+    for s in range(top - 1):
+        fill(s)
+    for t in range(2):
+        fill_weight(t)
+    after_y(1)
+    term(top, 1).start()
+    near_tap(1, 1).start()
+    for t in range(2, KH):
+        fill_weight(t)
+    start_all(wg_first)
+    add_on(0)
+    for t in range(KH, K + 1):
+        fill_weight(t)
+    start_all(wg_second)
     wg_recv[d] = wg_send[d]
-    start_all(wg_copy)
-    for t in near:
-        fill(t)
-    forward_far(1)
+    iacc[...] = mm_nt(gp_v[...], w_v[0])
     after_scatter(1)
-    half_tap(1, 1).start()
-    for t in near:
-        tap(1, t).start()
-    iacc[...] = mm_nt(gp_v[...], w_v[0])
-    for t in (1, 2):
-        wait_tap(1, t)
-        iacc[...] += taps[1, t - 1].astype(F32)
+    for q in range(2, NQ):
+        term(top, q).start()
+    for s in range(top - 1):
+        for q in range(NQ):
+            term(s, q).start()
+    add_on(1)
+    when_early(1, add_on, (2, 3))
     after_gather(1)
+    when_late(1, add_on, (2,))
+    after_gather_y(1)
+    when_late(1, add_on, (3,))
+    after_gather_core(1)
     left_send[...] = mm_tn(tok_v[...], lat[1]).astype(BF16).reshape(ND, RB, R)
     left_recv[d] = left_send[d]
     start_all(ls_copy)
     iacc[...] += mm_nt(lat[1], left_v[...])
-    receive_all(wg_copy)
+    for k in range(2):
+        near_tap(1, k).wait_recv()
+        iacc[...] += near_in[k].astype(F32)
+    receive_all(wg_first)
+    receive_all(wg_second)
 
     @pl.loop(0, K + 1)
     def _(t):
@@ -373,43 +442,66 @@
     left_out[...] = total.astype(BF16)
     lg_all[d] = left_out[...]
     start_all(lg_copy)
-    for t in near[::-1] + [second]:
-        wait_tap(1, t)
-        iacc[...] += taps[1, t - 1].astype(F32)
+    for s in range(top - 1):
+        for q in range(NQ):
+            term(s, q).wait_recv()
+        iacc[...] += chain_in[s].astype(F32)
+    for q in range(NQ):
+        term(top - 1, q).wait_recv()
+        rows = rows_of(q)
+        ig_v[rows] = (iacc[rows] + chain_in[top - 1, rows].astype(F32)).astype(BF16)
+    stores.append(pltpu.make_async_copy(ig_v, ig_h, local.at[9]))
+    stores[-1].start()
     receive_all(rg_copy)
     stores.append(pltpu.make_async_copy(rg_all, rg_h, local.at[7]))
     stores[-1].start()
+    for ph in range(2):
+        for copy in (ar_core, ar_y, ag_y, ag_core):
+            copy(ph).wait_send()
+        for k in range(2):
+            near_tap(ph, k).wait_send()
+
+        @pl.loop(1, Z)
+        def _(k):
+            z_scatter(ph, k).wait_send()
+            z_gather(ph, k).wait_send()
+
+    @pl.loop(1, ND)
+    def _(k):
+        for copy in (wg_first, wg_second, rg_copy, ls_copy):
+            copy(k).wait_send()
+
+    for q in range(NQ):
+        for s in range(top):
+            z_tap(s, q).wait_send()
+        z_pass(q).wait_send()
+        for s in range(nz):
+            term(s, q).wait_send()
+
     receive_all(lg_copy)
     stores.append(pltpu.make_async_copy(lg_all, lg_h, local.at[8]))
     stores[-1].start()
-    wait_tap(1, top)
-    ig_v[...] = (iacc[...] + taps[1, top - 1].astype(F32)).astype(BF16)
-    stores.append(pltpu.make_async_copy(ig_v, ig_h, local.at[9]))
-    stores[-1].start()
-
-    for ph in range(2):
-        for copy in (ar_core, ar_y, ag_y, ag_core):
-            copy(ph).wait_send()
-        for up in (True, False):
-            leg(ph, up).wait_send()
-            far(ph, up).wait_send()
-        for which in range(2):
-            half_tap(ph, which).wait_send()
-        for t in [1, 2] + near:
-            tap(ph, t).wait_send()
-
-        @pl.loop(1, Z)
-        def _(k):
-            z_scatter(ph, k).wait_send()
-            z_gather(ph, k).wait_send()
 
     @pl.loop(1, ND)
     def _(k):
-        for copy in (wg_copy, rg_copy, ls_copy, lg_copy):
-            copy(k).wait_send()
+        lg_copy(k).wait_send()
 
     for store in stores:
         store.wait()
+
+
+def hand_over(*refs):
+    n = (len(refs) - 1) // 3
+    ins, outs, held, sems = refs[:n], refs[n : 2 * n], refs[2 * n : 3 * n], refs[-1]
+    load = [pltpu.make_async_copy(ins[i], held[i], sems.at[0, i]) for i in range(n)]
+    store = [pltpu.make_async_copy(held[i], outs[i], sems.at[1, i]) for i in range(n)]
+    for copy in load:
+        copy.start()
+    for i in range(n):
+        load[i].wait()
+        store[i].start()
+    for copy in store:
+        copy.wait()
 
 
 def on_device(tokens, block_weight, left_factor, right_factor, out_cotangent):
@@ -432,18 +524,28 @@
         scratch_shapes=[
             bf(T, C), bf(K, C, H), bf(C, R), bf(R, H), bf(T, H),
             fl(T, H), bf(T, H), bf(T, H),
-            fl(2, 2, T // 2, R), fl(2, T // 2, R), fl(2, 2, T // 4, R), fl(2, T // 4, R),
+            fl(2, 2, T // 2, R), fl(2, T // 2, R), fl(2, 2, T // 4, R), bf(2, 2, T // 4, R), bf(2, T // 4, R),
             bf(2, Z, 16, 128), bf(2, Z, 16, 128), bf(2, 2, 2, Z, 16, 128), bf(2, T, R),
-            bf(2, K - 1, T, C), bf(K - 1, T, C), bf(2, 2, T // 2, C), fl(T, C), bf(T, C),
+            bf(K - 1, T, C), bf(2, T, C), bf(2, T, C),
+            fl(T, C), bf(K - 3, T, C), bf(K - 3, T, C), fl(T, C), bf(T, C),
             bf(ND, K + 1, RB, H), bf(ND, K + 1, RB, H), bf(K + 1, RB, H), bf(ND, RB, H),
             bf(ND, RB, R), bf(ND, RB, R), bf(RB, R), bf(ND, RB, R),
-            dma(2, TAP + K - 1), dma(2, TAP + K - 1), dma(2, 2, Z), dma(2, 2, Z),
-            dma(4, ND), dma(4, ND), dma(10),
+            dma(2, 6), dma(2, 6), dma(2, 2, Z), dma(2, 2, Z),
+            dma(K - 3, NQ), dma(K - 3, NQ), dma(K - 3, NQ), dma(K - 3, NQ),
+            dma(5, ND), dma(5, ND), dma(10),
         ],
         compiler_params=pltpu.CompilerParams(
             collective_id=0, has_side_effects=True, vmem_limit_bytes=56 * 1024 * 1024
         ),
     )(tokens, block_weight, left_factor, right_factor, out_cotangent)
+    results = (act, ig, wg, lg, rg)
+    act, ig, wg, lg, rg = pl.pallas_call(
+        hand_over,
+        out_shape=tuple(out(*x.shape) for x in results),
+        in_specs=[any_spec] * 5,
+        out_specs=[any_spec] * 5,
+        scratch_shapes=[bf(*x.shape) for x in results] + [dma(2, 5)],
+    )(*results)
     return act, ig, wg, lg.reshape(C, R), rg.reshape(R, H)
 
 

time: 154 us -> 133 us (0.86)
  the two profiles are of different devices: /device:TPU:1 before, /device:TPU:55 now
where the time goes in v2:
time: 133 us
  Pallas kernels  132 us (99%)
    pallas_call x1, Pallas kernels, on_device(): pl.pallas_call(functools.partial(kernel, Z, ND), out_shape=(out(T, H), ou...  130 us

profile of v2, /device:TPU:55, one launch (start us, length us, event | category | flops | bytes accessed | tf_op | source)
XLA Modules:
  0.0 132.5 jit_solution(5011981174300189162)
XLA Ops:
  0.6 129.7 %shard_map.92 = (bf16[512,512]{1,0:T(8,128)(2,1)}, bf16[512,256]{1,0:T(8,128)(2,1)}, bf16[7,32,512]{2,1,0:T(8,128)(2,1)}, bf16[8,32,256]{2,1,0:T(8,128)(2,1)}, bf16[8,32,512]{2,1,0:T(8,128)(2,1)}) custom-call(bf16[512,256]{1,0:T(8,128)(2,1)} %tok_h.1, bf16[7,256,512]{2,1,0:T(8,128)(2,1)} %w_h.1, bf16[256,256]{1,0:T(8,128)(2,1)} %left_h.1, ...), custom_call_target="tpu_custom_call" | custom-call | tf_op jit(solution)/shard_map/pallas_call | solution.py:519
  130.3 2.2 %shard_map.93 = (bf16[512,512]{1,0:T(8,128)(2,1)}, bf16[512,256]{1,0:T(8,128)(2,1)}, bf16[7,32,512]{2,1,0:T(8,128)(2,1)}, bf16[8,32,256]{2,1,0:T(8,128)(2,1)}, bf16[8,32,512]{2,1,0:T(8,128)(2,1)}) custom-call(bf16[512,512]{1,0:T(8,128)(2,1)} %get-tuple-element.15.refs_0_, bf16[512,256]{1,0:T(8,128)(2,1)} %get-tuple-element.16.refs_1_, ...), custom_call_target="tpu_custom_call" | custom-call | tf_op jit(solution)/shard_map/pallas_call | solution.py:542

commit v3 on v2

--- a/solution.py
+++ b/solution.py
@@ -12,7 +12,7 @@
 F32 = jnp.float32
 BF16 = jnp.bfloat16
 
-AR_CORE, AR_Y, AG_Y, AG_CORE, TAP_CORE, TAP_Y = range(6)
+AR_CORE, AR_Y, TAP_CORE, TAP_Y = range(4)
 NQ = 4
 
 
@@ -47,7 +47,7 @@
     part, rx_core, half, half_send, rx_y, z_send, z_recv, gathered, lat,
     taps, near_out, near_in, own, chain_out, chain_in, iacc, ig_v,
     wg_send, wg_recv, wg_out, rg_all, left_send, left_recv, left_out, lg_all,
-    one_send, one_recv, zs_send, zs_recv, f_send, f_recv, b_send, b_recv, d_send, d_recv, local,
+    one_send, one_recv, zs_send, zs_recv, g_send, g_recv, f_send, f_recv, b_send, b_recv, d_send, d_recv, local,
 ):
     T, C = tok_v.shape
     R, H = right_v.shape
@@ -71,6 +71,10 @@
     def z_at(k):
         return base + 4 * lax.rem(z + k, Z)
 
+    def by_distance(i):
+        odd = lax.rem(i, 2)
+        return odd * lax.div(i + 1, 2) + (1 - odd) * (Z - lax.div(i, 2))
+
     core_peer, y_peer = flip(1), flip(2)
 
     def to(src, dst, send, recv, **where):
@@ -113,11 +117,14 @@
     def ar_y(ph):
         return one(ph, AR_Y, half_send.at[ph, 1 - y], rx_y.at[ph], y_peer)
 
-    def ag_y(ph):
-        return one(ph, AG_Y, gathered.at[ph, c, y], gathered.at[ph, c, y], y_peer)
-
-    def ag_core(ph):
-        return one(ph, AG_CORE, gathered.at[ph, c], gathered.at[ph, c], core_peer)
+    def ag_y(ph, p, incoming=False):
+        piece = gathered.at[ph, c, 1 - y if incoming else y, p]
+        return to(piece, piece, g_send.at[ph, 0, p], g_recv.at[ph, 0, p], mp=y_peer)
+
+    def ag_core(ph, own_y, p, incoming=False):
+        piece = gathered.at[ph, 1 - c if incoming else c, y if own_y else 1 - y, p]
+        row = 1 if own_y else 2
+        return to(piece, piece, g_send.at[ph, row, p], g_recv.at[ph, row, p], mp=core_peer)
 
     def z_scatter(ph, k):
         there = lax.rem(z + k, Z)
@@ -215,7 +222,7 @@
 
         @pl.loop(1, Z)
         def _(k):
-            z_scatter(ph, k).start()
+            z_scatter(ph, by_distance(Z - k)).start()
 
     def after_scatter(ph):
         @pl.loop(1, Z)
@@ -229,21 +236,38 @@
 
         @pl.loop(1, Z)
         def _(k):
-            z_gather(ph, k).start()
+            z_gather(ph, by_distance(Z - k)).start()
+
+    def piece_at(i):
+        return lax.rem(z + by_distance(i), Z)
 
     def after_gather(ph):
+        ag_y(ph, z).start()
+        ag_core(ph, True, z).start()
+
         @pl.loop(1, Z)
-        def _(k):
-            z_gather_in(ph, k).wait_recv()
-
-        ag_y(ph).start()
+        def _(i):
+            z_gather_in(ph, by_distance(i)).wait_recv()
+            ag_y(ph, piece_at(i)).start()
+            ag_core(ph, True, piece_at(i)).start()
 
     def after_gather_y(ph):
-        one(ph, AG_Y, gathered.at[ph, c, 1 - y], gathered.at[ph, c, 1 - y], y_peer).wait_recv()
-        ag_core(ph).start()
+        def onward_core(p):
+            ag_y(ph, p, True).wait_recv()
+            ag_core(ph, False, p).start()
+
+        onward_core(z)
+
+        @pl.loop(1, Z)
+        def _(i):
+            onward_core(piece_at(i))
 
     def after_gather_core(ph):
-        one(ph, AG_CORE, gathered.at[ph, 1 - c], gathered.at[ph, 1 - c], core_peer).wait_recv()
+        @pl.loop(0, Z)
+        def _(p):
+            ag_core(ph, True, p, True).wait_recv()
+            ag_core(ph, False, p, True).wait_recv()
+
         for i in range(2):
             for j in range(2):
                 for rb in range(T4 // 16):
@@ -258,55 +282,49 @@
     part[0, 0] = partial[:T2]
     part[0, 1] = partial[T2:]
     pl.semaphore_wait(barrier, Z - 1 + ND - 1 + 2)
-    inner = way(z, top - 2) + way(z, top - 1) - 2 * way(z, top - 2) * way(z, top - 1)
-
-    def when_early(ph, queue, quarters):
-        @pl.when(inner == 1 - ph)
-        def _():
-            for q in quarters:
-                queue(q)
-
-    def when_late(ph, queue, quarters):
-        when_early(1 - ph, queue, quarters)
-
     ar_core(0).start()
     z_tap(top - 1, 0).start()
+    for q in range(2):
+        z_tap(0, q).start()
     after_core(0)
     near_tap(0, 0).start()
     loads[2].wait()
     acc[...] = mm(tok_v[...], w_v[0])
     after_y(0)
     z_tap(top - 1, 1).start()
+    for q in range(2, NQ):
+        z_tap(0, q).start()
     near_tap(0, 1).start()
     pass_on(0)
     after_scatter(0)
     for q in range(2, NQ):
         z_tap(top - 1, q).start()
-    for s in range(top - 1):
-        for q in range(NQ):
-            z_tap(s, q).start()
     pass_on(1)
     for k in range(2):
         near_tap(0, k).wait_recv()
         acc[...] += mm(taps[k], w_v[1 + k])
-    when_early(0, pass_on, (2, 3))
+    pass_on(2)
+    for q in range(NQ):
+        for s in range(1, top - 1):
+            z_tap(s, q).start()
+    pass_on(3)
     after_gather(0)
-    when_late(0, pass_on, (2,))
     loads[3].wait()
     loads[4].wait()
     after_gather_y(0)
-    when_late(0, pass_on, (3,))
     acc[...] += mm(taps[1 + top], w_v[2 + top])
+    for q in range(NQ):
+        arrived(0, q)
+    acc[...] += mm(taps[2], w_v[3])
     after_gather_core(0)
     acc[...] += mm(lat[0], right_v[...])
-    for s in range(top - 1):
-        for q in range(NQ):
+
+    stores = []
+    for q in range(NQ):
+        rows = rows_of(q)
+        for s in range(1, top - 1):
             arrived(s, q)
-        acc[...] += mm(taps[2 + s], w_v[3 + s])
-
-    stores = []
-    for q in range(NQ):
-        rows = rows_of(q)
+            acc[rows] += mm(taps[2 + s, rows], w_v[3 + s])
         arrived(top, q)
         acc[rows] += mm(taps[2 + top, rows], w_v[3 + top])
 
@@ -391,6 +409,8 @@
         fill_weight(t)
     after_y(1)
     term(top, 1).start()
+    for q in range(NQ):
+        term(0, q).start()
     near_tap(1, 1).start()
     for t in range(2, KH):
         fill_weight(t)
@@ -404,23 +424,19 @@
     after_scatter(1)
     for q in range(2, NQ):
         term(top, q).start()
-    for s in range(top - 1):
-        for q in range(NQ):
+    add_on(1)
+    add_on(2)
+    for q in range(NQ):
+        for s in range(1, top - 1):
             term(s, q).start()
-    add_on(1)
-    when_early(1, add_on, (2, 3))
+    add_on(3)
     after_gather(1)
-    when_late(1, add_on, (2,))
     after_gather_y(1)
-    when_late(1, add_on, (3,))
     after_gather_core(1)
     left_send[...] = mm_tn(tok_v[...], lat[1]).astype(BF16).reshape(ND, RB, R)
     left_recv[d] = left_send[d]
     start_all(ls_copy)
     iacc[...] += mm_nt(lat[1], left_v[...])
-    for k in range(2):
-        near_tap(1, k).wait_recv()
-        iacc[...] += near_in[k].astype(F32)
     receive_all(wg_first)
     receive_all(wg_second)
 
@@ -442,6 +458,9 @@
     left_out[...] = total.astype(BF16)
     lg_all[d] = left_out[...]
     start_all(lg_copy)
+    for k in range(2):
+        near_tap(1, k).wait_recv()
+        iacc[...] += near_in[k].astype(F32)
     for s in range(top - 1):
         for q in range(NQ):
             term(s, q).wait_recv()
@@ -456,7 +475,7 @@
     stores.append(pltpu.make_async_copy(rg_all, rg_h, local.at[7]))
     stores[-1].start()
     for ph in range(2):
-        for copy in (ar_core, ar_y, ag_y, ag_core):
+        for copy in (ar_core, ar_y):
             copy(ph).wait_send()
         for k in range(2):
             near_tap(ph, k).wait_send()
@@ -465,6 +484,12 @@
         def _(k):
             z_scatter(ph, k).wait_send()
             z_gather(ph, k).wait_send()
+
+        @pl.loop(0, Z)
+        def _(p):
+            ag_y(ph, p).wait_send()
+            ag_core(ph, True, p).wait_send()
+            ag_core(ph, False, p).wait_send()
 
     @pl.loop(1, ND)
     def _(k):
@@ -491,15 +516,11 @@
 
 
 def hand_over(*refs):
-    n = (len(refs) - 1) // 3
-    ins, outs, held, sems = refs[:n], refs[n : 2 * n], refs[2 * n : 3 * n], refs[-1]
-    load = [pltpu.make_async_copy(ins[i], held[i], sems.at[0, i]) for i in range(n)]
-    store = [pltpu.make_async_copy(held[i], outs[i], sems.at[1, i]) for i in range(n)]
-    for copy in load:
+    n = len(refs) // 2
+    sems = refs[-1]
+    store = [pltpu.make_async_copy(refs[i], refs[n + i], sems.at[i]) for i in range(n)]
+    for copy in store:
         copy.start()
-    for i in range(n):
-        load[i].wait()
-        store[i].start()
     for copy in store:
         copy.wait()
 
@@ -519,7 +540,7 @@
     act, ig, wg, lg, rg = pl.pallas_call(
         functools.partial(kernel, Z, ND),
         out_shape=(out(T, H), out(T, C), out(K, RB, H), out(ND, RB, R), out(ND, RB, H)),
-        in_specs=[any_spec] * 5,
+        in_specs=[pl.BlockSpec(memory_space=pltpu.HBM)] * 5,
         out_specs=[any_spec] * 5,
         scratch_shapes=[
             bf(T, C), bf(K, C, H), bf(C, R), bf(R, H), bf(T, H),
@@ -530,21 +551,22 @@
             fl(T, C), bf(K - 3, T, C), bf(K - 3, T, C), fl(T, C), bf(T, C),
             bf(ND, K + 1, RB, H), bf(ND, K + 1, RB, H), bf(K + 1, RB, H), bf(ND, RB, H),
             bf(ND, RB, R), bf(ND, RB, R), bf(RB, R), bf(ND, RB, R),
-            dma(2, 6), dma(2, 6), dma(2, 2, Z), dma(2, 2, Z),
+            dma(2, 4), dma(2, 4), dma(2, 2, Z), dma(2, 2, Z), dma(2, 3, Z), dma(2, 3, Z),
             dma(K - 3, NQ), dma(K - 3, NQ), dma(K - 3, NQ), dma(K - 3, NQ),
             dma(5, ND), dma(5, ND), dma(10),
         ],
         compiler_params=pltpu.CompilerParams(
-            collective_id=0, has_side_effects=True, vmem_limit_bytes=56 * 1024 * 1024
+            collective_id=0, has_side_effects=True, vmem_limit_bytes=26 * 1024 * 1024
         ),
-    )(tokens, block_weight, left_factor, right_factor, out_cotangent)
+    )(*[pltpu.with_memory_space_constraint(v, pltpu.HBM) for v in (tokens, block_weight, left_factor, right_factor, out_cotangent)])
     results = (act, ig, wg, lg, rg)
     act, ig, wg, lg, rg = pl.pallas_call(
         hand_over,
         out_shape=tuple(out(*x.shape) for x in results),
-        in_specs=[any_spec] * 5,
-        out_specs=[any_spec] * 5,
-        scratch_shapes=[bf(*x.shape) for x in results] + [dma(2, 5)],
+        in_specs=[pl.BlockSpec(memory_space=pltpu.VMEM)] * 5,
+        out_specs=[pl.BlockSpec(memory_space=pltpu.HBM)] * 5,
+        scratch_shapes=[dma(5)],
+        compiler_params=pltpu.CompilerParams(vmem_limit_bytes=4 * 1024 * 1024),
     )(*results)
     return act, ig, wg, lg.reshape(C, R), rg.reshape(R, H)
 

time: 133 us -> 128 us (0.962)
  the two profiles are of different devices: /device:TPU:55 before, /device:TPU:1 now
where the time goes in v3:
time: 128 us
  Pallas kernels  127 us (99%)
    pallas_call x1, Pallas kernels, on_device(): pl.pallas_call(functools.partial(kernel, Z, ND), out_shape=(out(T, H), ou...  126 us

profile of v3, /device:TPU:1, one launch (start us, length us, event | category | flops | bytes accessed | tf_op | source)
XLA Modules:
  0.0 127.8 jit_solution(11308821448239109394)
XLA Ops:
  0.6 126.0 %shard_map.92 = (bf16[512,512]{1,0:T(8,128)(2,1)S(1)}, bf16[512,256]{1,0:T(8,128)(2,1)S(1)}, bf16[7,32,512]{2,1,0:T(8,128)(2,1)S(1)}, bf16[8,32,256]{2,1,0:T(8,128)(2,1)S(1)}, bf16[8,32,512]{2,1,0:T(8,128)(2,1)S(1)}) custom-call(bf16[512,256]{1,0:T(8,128)(2,1)} %tok_h.1, bf16[7,256,512]{2,1,0:T(8,128)(2,1)} %w_h.1, bf16[256,256]{1,0:T(8,128)(2,1)} %left_h.1, ...), custom_call_target="tpu_custom_call" | custom-call | tf_op jit(solution)/shard_map/pallas_call | solution.py:540
  126.6 1.1 shard_map.93

commit v4 on v3

--- a/solution.py
+++ b/solution.py
@@ -276,16 +276,16 @@
                             gathered[ph, i, j, rb * NC + ch]
                         )
 
+    pl.semaphore_wait(barrier, Z - 1 + ND - 1 + 2)
+    z_tap(top - 1, 0).start()
+    for q in range(2):
+        z_tap(0, q).start()
     loads[0].wait()
     loads[1].wait()
     partial = mm(tok_v[...], left_v[...])
     part[0, 0] = partial[:T2]
     part[0, 1] = partial[T2:]
-    pl.semaphore_wait(barrier, Z - 1 + ND - 1 + 2)
     ar_core(0).start()
-    z_tap(top - 1, 0).start()
-    for q in range(2):
-        z_tap(0, q).start()
     after_core(0)
     near_tap(0, 0).start()
     loads[2].wait()

time: 128 us -> 134 us (1.047)
  the two profiles are of different devices: /device:TPU:1 before, /device:TPU:57 now
where the time goes in v4:
time: 134 us
  Pallas kernels  133 us (99%)
    pallas_call x1, Pallas kernels, on_device(): pl.pallas_call(functools.partial(kernel, Z, ND), out_shape=(out(T, H), ou...  132 us

profile of v4, /device:TPU:57, one launch (start us, length us, event | category | flops | bytes accessed | tf_op | source)
XLA Modules:
  0.0 133.7 jit_solution(18119579247262012585)
XLA Ops:
  0.6 131.9 %shard_map.92 = (bf16[512,512]{1,0:T(8,128)(2,1)S(1)}, bf16[512,256]{1,0:T(8,128)(2,1)S(1)}, bf16[7,32,512]{2,1,0:T(8,128)(2,1)S(1)}, bf16[8,32,256]{2,1,0:T(8,128)(2,1)S(1)}, bf16[8,32,512]{2,1,0:T(8,128)(2,1)S(1)}) custom-call(bf16[512,256]{1,0:T(8,128)(2,1)} %tok_h.1, bf16[7,256,512]{2,1,0:T(8,128)(2,1)} %w_h.1, bf16[256,256]{1,0:T(8,128)(2,1)} %left_h.1, ...), custom_call_target="tpu_custom_call" | custom-call | tf_op jit(solution)/shard_map/pallas_call | solution.py:540
  132.6 1.1 shard_map.93
